TPU v7x, 256 devices: a whole 4x4x8 slice. The times are simulated.
256 devices in a mesh: corpus: 64 (over y, z, x_hi), vocab: 4 (over x_lo, core).
Axes of the slice: x: 4 (x_hi: 2, x_lo: 2; x = x_hi * 2 + x_lo), y: 4, z: 8, core: 2. Of those that a mesh axis runs over, the one named last changes fastest.
Arguments:
- eval_tiles: bfloat16 [64, 12, 128, 512], P('corpus', 'vocab'), may hold values from 0.019897461 to 2
- eval_tile_list: int32 [64, 12], P(None, 'vocab'), may hold values from 0 to 128, as said below
- corpus_tiles: bfloat16 [256, 12, 128, 512], P('corpus', 'vocab'), may hold values from 0.019897461 to 2
- corpus_tile_list: int32 [256, 12], P('corpus', 'vocab'), may hold values from 0 to 128, as said below
- pair_eval_block: int32 [6144], P('corpus'), may hold values from 0 to 63
- pair_corpus_block: int32 [6144], P('corpus'), may hold values from 0 to 3
- pair_count: int32 [64], P('corpus'), may hold values from 12 to 96, as said below
- eval_norm: float32 [8192], replicated, may hold values from 8 to 32
- corpus_norm: float32 [32768], P('corpus'), may hold values from 8 to 32
Outputs:
- cosine_tiles: float32 [6144, 128, 128], P(('corpus', 'vocab'))
Inputs may be any that keep to these rules, and one draw needn't show every extreme that they name: `eval_tile_list`: value 128 marks an empty slot; other ids of one row block in one slice are distinct. Slot 0 of a block and slice is never empty. `corpus_tile_list`: value 128 marks an empty slot; other ids of one row block in one slice are distinct. Slot 0 of a block and slice is never empty. Shard c's live pair slots are its first pair_count[c] slots. Some shard is full.
All inputs are finite; a program needn't handle non-finite values.
Results may differ from a plain program's by a relative error of at most 0.0003.
Values may be sent and summed in bfloat16 or wider, within the bound.
A program may use at most 128 MiB of HBM per device.

v0:
```python
import jax
import jax.numpy as jnp
from jax import lax
from jax.sharding import PartitionSpec as P

VOCAB = 262144
GROUP = 8


def local(
    eval_tiles,
    eval_tile_list,
    corpus_tiles,
    corpus_tile_list,
    pair_eval_block,
    pair_corpus_block,
    pair_count,
    eval_norm,
    corpus_norm,
):
    slices = lax.axis_size("vocab")
    term_width = corpus_tiles.shape[3]
    tile_rows = corpus_tiles.shape[2]
    tiles_slice = VOCAB // (term_width * slices)
    pair_slots = pair_eval_block.shape[0]
    quarter = pair_slots // slices
    every_eval = lax.all_gather(eval_tiles, "corpus", axis=0, tiled=True)
    position = jnp.arange(pair_slots, dtype=jnp.int32)
    own_live = position < pair_count[0]
    groups = quarter * lax.axis_size("vocab") // GROUP

    def one_group(group_index, totals):
        first_slot = group_index * GROUP
        living = lax.dynamic_slice_in_dim(own_live, first_slot, GROUP)

        def compute(current):
            eval_index = lax.dynamic_slice_in_dim(pair_eval_block, first_slot, GROUP)
            block_index = lax.dynamic_slice_in_dim(pair_corpus_block, first_slot, GROUP)
            eval_part = every_eval[eval_index]
            eval_list = eval_tile_list[eval_index]
            corpus_part = corpus_tiles[block_index]
            corpus_list = corpus_tile_list[block_index]
            matched = (eval_list[:, :, None] == corpus_list[:, None, :]) & (
                eval_list[:, :, None] < tiles_slice
            )
            aligned = jnp.einsum(
                "gij,gjrt->girt",
                matched.astype(jnp.bfloat16),
                corpus_part,
                preferred_element_type=jnp.float32,
            ).astype(jnp.bfloat16)
            products = jnp.einsum(
                "girt,gist->grs", eval_part, aligned, preferred_element_type=jnp.float32
            )
            products = jnp.where(living[:, None, None], products, 0.0)
            return lax.dynamic_update_slice_in_dim(current, products, group_index * GROUP, 0)

        return lax.cond(jnp.any(living), compute, lambda current: current, totals)

    start_totals = jnp.zeros((quarter * lax.axis_size("vocab"), tile_rows, tile_rows), jnp.float32)
    summed = lax.psum_scatter(
        lax.fori_loop(0, groups, one_group, start_totals), "vocab", scatter_dimension=0, tiled=True
    )
    vocab_index = lax.axis_index("vocab")
    first_pair = vocab_index * quarter
    mine_eval = lax.dynamic_slice_in_dim(pair_eval_block, first_pair, quarter)
    mine_block = lax.dynamic_slice_in_dim(pair_corpus_block, first_pair, quarter)
    mine_live = lax.dynamic_slice_in_dim(own_live, first_pair, quarter)
    eval_scale = eval_norm.reshape(-1, tile_rows)[mine_eval]
    corpus_scale = corpus_norm.reshape(-1, tile_rows)[mine_block]
    cosine = summed / (eval_scale[:, :, None] * corpus_scale[:, None, :])
    return jnp.where(mine_live[:, None, None], cosine, 0.0)


def solution(mesh):
    in_specs = (
        P("corpus", "vocab", None, None),
        P(None, "vocab"),
        P("corpus", "vocab", None, None),
        P("corpus", "vocab"),
        P("corpus"),
        P("corpus"),
        P("corpus"),
        P(),
        P("corpus"),
    )
    out_specs = P(("corpus", "vocab"), None, None)
    return jax.shard_map(local, mesh=mesh, in_specs=in_specs, out_specs=out_specs, check_vma=False)
```

profile of v0, /device:TPU:1, one launch (start us, length us, event | category | flops | bytes accessed | tf_op | source)
XLA Modules:
  0.0 635.2 jit_solution(17635871114623681145)
XLA Ops:
  8.0 0.8 copy.11
  8.8 279.0 %all-gather.2.cloned.1.call-done = bf16[64,3,128,512]{3,2,1,0:T(8,128)(2,1)} async-done(((bf16[1,3,128,512]{3,2,1,0:T(8,128)(2,1)}), bf16[64,3,128,512]{3,2,1,0:T(8,128)(2,1)}) %all-gather.2.cloned.1.call-update) | async-done | bytes 25165840 | tf_op jit(solution)/shard_map/all_gather | solution.py:27
  287.8 3.5 broadcast_in_dim.49
  291.3 145.8 %while.16 = (s32[]{:T(128)}, f32[96,128,128]{2,1,0:T(8,128)}, pred[96]{0:T(512)(128)(4,1)S(1)}, s32[96]{0:T(128)S(1)}, bf16[64,3,128,512]{3,2,1,0:T(8,128)(2,1)}...) while((s32[]{:T(128)}, f32[96,128,128]{2,1,0:T(8,128)}, ...), condition=%wide.region_4.5_spmd, body=%wide.region_0.4_spmd.sunk | while | flops 412223712 | bytes 38282672 | solution.py:62
  291.3 0.8 fusion.15
  292.8 21.3 %conditional.2 = (f32[96,128,128]{2,1,0:T(8,128)}) conditional(s32[]{:T(128)} %convert_element_type.20, f32[96,128,128]{2,1,0:T(8,128)} %get-tuple-element.313, (pred[8]{0:T(512)(128)(4,1)S(1)}, s32[]{:T(128)}, s32[96]{0:T(128)S(1)}, bf16[64,3,128,512]{3,2,1,0:T(8,128)(2,1)}, s32[64,3]{1,0:T(8,128)S(1)}, /*index=5*/s32[96]{0:T(128)S(1)}, ...), branch_computations={%region_2.0_spmd, %region_3.3_spmd} | conditional | flops 412223712 | bytes 38282388 | solution.py:58
  292.9 10.5 %gather_fusion = bf16[8,3,128,512]{3,2,1,0:T(8,128)(2,1)} fusion(bf16[64,3,128,512]{3,2,1,0:T(8,128)(2,1)} %get-tuple-element.178, s32[1024]{0:T(1024)S(1)} %pad_clamp_fusion.1), kind=kCustom, calls=%fused_computation | custom fusion | bytes 6291488 | tf_op jit(solution)/shard_map/while/body/eval_jaxpr/cond/branch_1_fun/gather | solution.py:39
  303.4 2.5 gather_fusion.3
  307.1 4.9 fusion
  312.0 2.1 fusion.5
  314.1 0.8 fusion.15
  315.6 21.3 %conditional.2 = (f32[96,128,128]{2,1,0:T(8,128)}) conditional(s32[]{:T(128)} %convert_element_type.20, f32[96,128,128]{2,1,0:T(8,128)} %get-tuple-element.313, (pred[8]{0:T(512)(128)(4,1)S(1)}, s32[]{:T(128)}, s32[96]{0:T(128)S(1)}, bf16[64,3,128,512]{3,2,1,0:T(8,128)(2,1)}, s32[64,3]{1,0:T(8,128)S(1)}, /*index=5*/s32[96]{0:T(128)S(1)}, ...), branch_computations={%region_2.0_spmd, %region_3.3_spmd} | conditional | flops 412223712 | bytes 38282388 | solution.py:58
  315.7 10.5 %gather_fusion = bf16[8,3,128,512]{3,2,1,0:T(8,128)(2,1)} fusion(bf16[64,3,128,512]{3,2,1,0:T(8,128)(2,1)} %get-tuple-element.178, s32[1024]{0:T(1024)S(1)} %pad_clamp_fusion.1), kind=kCustom, calls=%fused_computation | custom fusion | bytes 6291488 | tf_op jit(solution)/shard_map/while/body/eval_jaxpr/cond/branch_1_fun/gather | solution.py:39
  326.2 2.5 gather_fusion.3
  329.9 4.9 fusion
  334.8 2.1 fusion.5
  336.9 0.8 fusion.15
  338.4 21.3 %conditional.2 = (f32[96,128,128]{2,1,0:T(8,128)}) conditional(s32[]{:T(128)} %convert_element_type.20, f32[96,128,128]{2,1,0:T(8,128)} %get-tuple-element.313, (pred[8]{0:T(512)(128)(4,1)S(1)}, s32[]{:T(128)}, s32[96]{0:T(128)S(1)}, bf16[64,3,128,512]{3,2,1,0:T(8,128)(2,1)}, s32[64,3]{1,0:T(8,128)S(1)}, /*index=5*/s32[96]{0:T(128)S(1)}, ...), branch_computations={%region_2.0_spmd, %region_3.3_spmd} | conditional | flops 412223712 | bytes 38282388 | solution.py:58
  338.5 10.5 %gather_fusion = bf16[8,3,128,512]{3,2,1,0:T(8,128)(2,1)} fusion(bf16[64,3,128,512]{3,2,1,0:T(8,128)(2,1)} %get-tuple-element.178, s32[1024]{0:T(1024)S(1)} %pad_clamp_fusion.1), kind=kCustom, calls=%fused_computation | custom fusion | bytes 6291488 | tf_op jit(solution)/shard_map/while/body/eval_jaxpr/cond/branch_1_fun/gather | solution.py:39
  349.0 2.5 gather_fusion.3
  352.7 4.9 fusion
  357.6 2.1 fusion.5
  359.7 0.8 fusion.15
  361.1 21.3 %conditional.2 = (f32[96,128,128]{2,1,0:T(8,128)}) conditional(s32[]{:T(128)} %convert_element_type.20, f32[96,128,128]{2,1,0:T(8,128)} %get-tuple-element.313, (pred[8]{0:T(512)(128)(4,1)S(1)}, s32[]{:T(128)}, s32[96]{0:T(128)S(1)}, bf16[64,3,128,512]{3,2,1,0:T(8,128)(2,1)}, s32[64,3]{1,0:T(8,128)S(1)}, /*index=5*/s32[96]{0:T(128)S(1)}, ...), branch_computations={%region_2.0_spmd, %region_3.3_spmd} | conditional | flops 412223712 | bytes 38282388 | solution.py:58
  361.3 10.5 %gather_fusion = bf16[8,3,128,512]{3,2,1,0:T(8,128)(2,1)} fusion(bf16[64,3,128,512]{3,2,1,0:T(8,128)(2,1)} %get-tuple-element.178, s32[1024]{0:T(1024)S(1)} %pad_clamp_fusion.1), kind=kCustom, calls=%fused_computation | custom fusion | bytes 6291488 | tf_op jit(solution)/shard_map/while/body/eval_jaxpr/cond/branch_1_fun/gather | solution.py:39
  371.8 2.5 gather_fusion.3
  375.4 4.9 fusion
  380.4 2.0 fusion.5
  382.4 0.8 fusion.15
  383.9 21.3 %conditional.2 = (f32[96,128,128]{2,1,0:T(8,128)}) conditional(s32[]{:T(128)} %convert_element_type.20, f32[96,128,128]{2,1,0:T(8,128)} %get-tuple-element.313, (pred[8]{0:T(512)(128)(4,1)S(1)}, s32[]{:T(128)}, s32[96]{0:T(128)S(1)}, bf16[64,3,128,512]{3,2,1,0:T(8,128)(2,1)}, s32[64,3]{1,0:T(8,128)S(1)}, /*index=5*/s32[96]{0:T(128)S(1)}, ...), branch_computations={%region_2.0_spmd, %region_3.3_spmd} | conditional | flops 412223712 | bytes 38282388 | solution.py:58
  384.0 10.5 %gather_fusion = bf16[8,3,128,512]{3,2,1,0:T(8,128)(2,1)} fusion(bf16[64,3,128,512]{3,2,1,0:T(8,128)(2,1)} %get-tuple-element.178, s32[1024]{0:T(1024)S(1)} %pad_clamp_fusion.1), kind=kCustom, calls=%fused_computation | custom fusion | bytes 6291488 | tf_op jit(solution)/shard_map/while/body/eval_jaxpr/cond/branch_1_fun/gather | solution.py:39
  394.6 2.5 gather_fusion.3
  398.2 4.9 fusion
  403.1 2.1 fusion.5
  405.2 0.8 fusion.15
  406.7 21.3 %conditional.2 = (f32[96,128,128]{2,1,0:T(8,128)}) conditional(s32[]{:T(128)} %convert_element_type.20, f32[96,128,128]{2,1,0:T(8,128)} %get-tuple-element.313, (pred[8]{0:T(512)(128)(4,1)S(1)}, s32[]{:T(128)}, s32[96]{0:T(128)S(1)}, bf16[64,3,128,512]{3,2,1,0:T(8,128)(2,1)}, s32[64,3]{1,0:T(8,128)S(1)}, /*index=5*/s32[96]{0:T(128)S(1)}, ...), branch_computations={%region_2.0_spmd, %region_3.3_spmd} | conditional | flops 412223712 | bytes 38282388 | solution.py:58
  406.8 10.5 %gather_fusion = bf16[8,3,128,512]{3,2,1,0:T(8,128)(2,1)} fusion(bf16[64,3,128,512]{3,2,1,0:T(8,128)(2,1)} %get-tuple-element.178, s32[1024]{0:T(1024)S(1)} %pad_clamp_fusion.1), kind=kCustom, calls=%fused_computation | custom fusion | bytes 6291488 | tf_op jit(solution)/shard_map/while/body/eval_jaxpr/cond/branch_1_fun/gather | solution.py:39
  417.3 2.5 gather_fusion.3
  421.0 4.9 fusion
  425.9 2.0 fusion.5
  428.0 0.8 fusion.15
  429.5 0.8 fusion.15
  431.0 0.8 fusion.15
  432.5 0.8 fusion.15
  434.1 0.8 fusion.15
  435.6 0.8 fusion.15
  438.9 186.3 %reduce-scatter.2.cloned.1.call-done = f32[24,128,128]{2,1,0:T(8,128)} async-done(((f32[96,128,128]{2,1,0:T(8,128)}), f32[24,128,128]{2,1,0:T(8,128)}) %reduce-scatter.2.cloned.1.call-update) | async-done | bytes 1572880 | tf_op jit(solution)/shard_map/reduce_scatter | solution.py:61
  625.3 3.1 divide_select_fusion
  (77 shorter events, 9.9 us)
Async XLA Ops:
  6.5 431.8 %copy-start = (f32[8192]{0:T(1024)S(1)}, f32[8192]{0:T(1024)}, u32[]{:S(2)}) copy-start(f32[8192]{0:T(1024)} %param.20) | copy-start | bytes 98308
  6.5 281.3 %all-gather.2.cloned.1.call-start = ((), (), s32[]{:S(2)}) async-start(), calls=%async_computation.1 | async-start | bytes 25559040 | tf_op jit(solution)/shard_map/all_gather | solution.py:27
  7.3 618.0 %reduce-scatter.2.cloned.1.call-start = ((), (), s32[]{:S(2)}) async-start(), calls=%async_computation.2 | async-start | bytes 7864320 | tf_op jit(solution)/shard_map/reduce_scatter | solution.py:61
  8.7 282.5 %copy-start.1 = (bf16[4,3,128,512]{3,2,1,0:T(8,128)(2,1)S(1)}, bf16[4,3,128,512]{3,2,1,0:T(8,128)(2,1)}, u32[]{:S(2)}) copy-start(bf16[4,3,128,512]{3,2,1,0:T(8,128)(2,1)} %param.15) | copy-start | bytes 4718596
  8.7 282.5 %copy-start.3 = (s32[4,3]{1,0:T(4,128)S(1)}, s32[4,3]{1,0:T(4,128)}, u32[]{:S(2)}) copy-start(s32[4,3]{1,0:T(4,128)} %param.16) | copy-start | bytes 148
  8.7 282.5 %copy-start.5 = (s32[96]{0:T(128)S(1)}, s32[96]{0:T(128)}, u32[]{:S(2)}) copy-start(s32[96]{0:T(128)} %param.17) | copy-start | bytes 1156
  8.8 282.5 %copy-start.6 = (s32[96]{0:T(128)S(1)}, s32[96]{0:T(128)}, u32[]{:S(2)}) copy-start(s32[96]{0:T(128)} %param.18) | copy-start | bytes 1156
  307.1 4.9 copy-start.2
  329.9 4.9 copy-start.2
  352.7 4.9 copy-start.2
  375.4 4.9 copy-start.2
  398.2 4.9 copy-start.2
  421.0 4.9 copy-start.2
  437.1 0.7 copy-start.4
Sparse Core Ops, SparseCore 0:
  11.0 276.7 all-gather.1
  437.3 187.9 reduce-scatter.1
where the time goes:
time: 636 us; the launch traced here: 635 us
  waiting for transfers between devices  466 us (73%)
  local copies, waits for them, and re-layouts  90.8 us (14%)
  matrix products  41.9 us (7%)
  between operations  14.1 us (2%)
  other arithmetic  13.2 us (2%)
  loops' own time  9.02 us (1%)
    all_gather x1, waiting for transfers between devices, local(): every_eval = lax.all_gather(eval_tiles, 'corpus', axis=0, tiled=True)  279 us
    reduce_scatter x1, waiting for transfers between devices, local(): lax.psum_scatter(lax.fori_loop(0, groups, one_group, start_totals), 'voca...  186 us
    gather x6, local copies, waits for them, and re-layouts, compute(): eval_part = every_eval[eval_index]  63.2 us
    dot_general x6, matrix products, compute(): jnp.einsum('gij,gjrt->girt', matched.astype(jnp.bfloat16), corpus_part, p...  29.5 us
    gather x6, local copies, waits for them, and re-layouts, compute(): corpus_part = corpus_tiles[block_index]  15 us
  transfers between devices with their start and end apart: 2, of which 2 were waited for; matrix products, arithmetic and copies ran while one was open for 0% of the time, Pallas kernels for 0%

commit v1 on v0

--- a/solution.py
+++ b/solution.py
@@ -24,7 +24,15 @@
     tiles_slice = VOCAB // (term_width * slices)
     pair_slots = pair_eval_block.shape[0]
     quarter = pair_slots // slices
-    every_eval = lax.all_gather(eval_tiles, "corpus", axis=0, tiled=True)
+    every_eval = jnp.concatenate(
+        lax.all_to_all(
+            jnp.stack(lax.axis_size("corpus") * [eval_tiles]),
+            axis_name="corpus",
+            split_axis=0,
+            concat_axis=0,
+        ),
+        axis=0,
+    )
     position = jnp.arange(pair_slots, dtype=jnp.int32)
     own_live = position < pair_count[0]
     groups = quarter * lax.axis_size("vocab") // GROUP

time: 636 us -> 1030 us (1.62)
  waiting for transfers between devices: 466 us -> 808 us
  matrix products: 41.9 us -> 71.6 us
  starting transfers between devices: 0.04 us -> 15.5 us
    all_to_all x0 -> x1, waiting for transfers between devices: none -> 592 us  [local(): lax.all_to_all(jnp.stack(lax.axis_size('corpus') * [eval_tiles]), axis_na...]
    all_gather x1 -> x0, waiting for transfers between devices: 279 us -> none  [local(): every_eval = lax.all_gather(eval_tiles, 'corpus', axis=0, tiled=True)]
    reduce_scatter x1, waiting for transfers between devices: 186 us -> 217 us  [local(): lax.psum_scatter(lax.fori_loop(0, groups, one_group, start_totals), 'voca...]
    dot_general x6, matrix products: 12.4 us -> 31.2 us  [compute(): jnp.einsum('girt,gist->grs', eval_part, aligned, preferred_element_type=j...]
    all_to_all x0 -> x1, starting transfers between devices: none -> 15.5 us  [local(): lax.all_to_all(jnp.stack(lax.axis_size('corpus') * [eval_tiles]), axis_na...]
    dot_general x6, matrix products: 29.5 us -> 40.4 us  [compute(): jnp.einsum('gij,gjrt->girt', matched.astype(jnp.bfloat16), corpus_part, p...]
where the time goes in v1:
time: 1030 us
  waiting for transfers between devices  808 us (78%)
  local copies, waits for them, and re-layouts  99.3 us (10%)
  matrix products  71.6 us (7%)
  starting transfers between devices  15.5 us (2%)
  between operations  14.1 us (1%)
  other arithmetic  13 us (1%)
    all_to_all x1, waiting for transfers between devices, local(): lax.all_to_all(jnp.stack(lax.axis_size('corpus') * [eval_tiles]), axis_na...  592 us
    reduce_scatter x1, waiting for transfers between devices, local(): lax.psum_scatter(lax.fori_loop(0, groups, one_group, start_totals), 'voca...  217 us
    gather x6, local copies, waits for them, and re-layouts, compute(): eval_part = every_eval[eval_index]  63.7 us
    dot_general x6, matrix products, compute(): jnp.einsum('gij,gjrt->girt', matched.astype(jnp.bfloat16), corpus_part, p...  40.4 us
    dot_general x6, matrix products, compute(): jnp.einsum('girt,gist->grs', eval_part, aligned, preferred_element_type=j...  31.2 us
  transfers between devices with their start and end apart: 2, of which 2 were waited for; matrix products, arithmetic and copies ran while one was open for 0% of the time, Pallas kernels for 0%

profile of v1, /device:TPU:1, one launch (start us, length us, event | category | flops | bytes accessed | tf_op | source)
XLA Modules:
  0.0 1030.1 jit_solution(9506784174704673060)
XLA Ops:
  6.5 9.4 stack.2
  16.0 15.5 %all-to-all-start = ((bf16[64,1,3,128,512]{4,3,2,1,0:T(8,128)(2,1)}), bf16[64,1,3,128,512]{4,3,2,1,0:T(8,128)(2,1)}, u32[]{:S(2)}, u32[]{:S(2)}) async-start(bf16[64,1,3,128,512]{4,3,2,1,0:T(8,128)(2,1)} %stack.2), calls=%async_computation | async-start | bytes 50331648 | tf_op jit(solution)/shard_map/all_to_all | solution.py:28
  32.3 591.5 %all-to-all-done = bf16[64,1,3,128,512]{4,3,2,1,0:T(8,128)(2,1)} async-done(((bf16[64,1,3,128,512]{4,3,2,1,0:T(8,128)(2,1)}), bf16[64,1,3,128,512]{4,3,2,1,0:T(8,128)(2,1)}, u32[]{:S(2)}, u32[]{:S(2)}) %all-to-all-start) | async-done | bytes 25165856 | tf_op jit(solution)/shard_map/all_to_all | solution.py:28
  623.8 3.5 broadcast_in_dim.49
  627.3 174.8 %while.16 = (s32[]{:T(128)}, f32[96,128,128]{2,1,0:T(8,128)}, pred[96]{0:T(512)(128)(4,1)S(1)}, s32[96]{0:T(128)S(1)}, bf16[64,3,128,512]{3,2,1,0:T(8,128)(2,1)}...) while((s32[]{:T(128)}, f32[96,128,128]{2,1,0:T(8,128)}, ...), condition=%wide.region_4.5_spmd, body=%wide.region_0.4_spmd.sunk | while | flops 412223712 | bytes 26748300 | solution.py:70
  627.3 0.8 fusion.15
  628.7 26.3 %conditional.2 = (f32[96,128,128]{2,1,0:T(8,128)}) conditional(s32[]{:T(128)} %convert_element_type.20, f32[96,128,128]{2,1,0:T(8,128)} %get-tuple-element.313, (pred[8]{0:T(512)(128)(4,1)S(1)}, s32[]{:T(128)}, s32[96]{0:T(128)S(1)}, bf16[64,3,128,512]{3,2,1,0:T(8,128)(2,1)}, s32[64,3]{1,0:T(8,128)S(1)}, /*index=5*/s32[96]{0:T(128)S(1)}, ...), branch_computations={%region_2.0_spmd, %region_3.3_spmd} | conditional | flops 412223712 | bytes 26748024 | solution.py:66
  629.4 2.5 gather_fusion.3
  632.4 6.7 fusion
  639.2 10.6 %gather_fusion = bf16[8,3,128,512]{3,2,1,0:T(8,128)(2,1)} fusion(bf16[64,3,128,512]{3,2,1,0:T(8,128)(2,1)} %get-tuple-element.178, s32[1024]{0:T(1024)S(1)} %pad_clamp_fusion.1), kind=kCustom, calls=%fused_computation | custom fusion | bytes 6291488 | tf_op jit(solution)/shard_map/while/body/eval_jaxpr/cond/branch_1_fun/gather | solution.py:47
  649.8 5.2 fusion.5
  655.0 0.8 fusion.15
  656.4 26.3 %conditional.2 = (f32[96,128,128]{2,1,0:T(8,128)}) conditional(s32[]{:T(128)} %convert_element_type.20, f32[96,128,128]{2,1,0:T(8,128)} %get-tuple-element.313, (pred[8]{0:T(512)(128)(4,1)S(1)}, s32[]{:T(128)}, s32[96]{0:T(128)S(1)}, bf16[64,3,128,512]{3,2,1,0:T(8,128)(2,1)}, s32[64,3]{1,0:T(8,128)S(1)}, /*index=5*/s32[96]{0:T(128)S(1)}, ...), branch_computations={%region_2.0_spmd, %region_3.3_spmd} | conditional | flops 412223712 | bytes 26748024 | solution.py:66
  657.1 2.5 gather_fusion.3
  660.1 6.7 fusion
  666.9 10.6 %gather_fusion = bf16[8,3,128,512]{3,2,1,0:T(8,128)(2,1)} fusion(bf16[64,3,128,512]{3,2,1,0:T(8,128)(2,1)} %get-tuple-element.178, s32[1024]{0:T(1024)S(1)} %pad_clamp_fusion.1), kind=kCustom, calls=%fused_computation | custom fusion | bytes 6291488 | tf_op jit(solution)/shard_map/while/body/eval_jaxpr/cond/branch_1_fun/gather | solution.py:47
  677.5 5.2 fusion.5
  682.7 0.8 fusion.15
  684.1 26.3 %conditional.2 = (f32[96,128,128]{2,1,0:T(8,128)}) conditional(s32[]{:T(128)} %convert_element_type.20, f32[96,128,128]{2,1,0:T(8,128)} %get-tuple-element.313, (pred[8]{0:T(512)(128)(4,1)S(1)}, s32[]{:T(128)}, s32[96]{0:T(128)S(1)}, bf16[64,3,128,512]{3,2,1,0:T(8,128)(2,1)}, s32[64,3]{1,0:T(8,128)S(1)}, /*index=5*/s32[96]{0:T(128)S(1)}, ...), branch_computations={%region_2.0_spmd, %region_3.3_spmd} | conditional | flops 412223712 | bytes 26748024 | solution.py:66
  684.8 2.5 gather_fusion.3
  687.8 6.7 fusion
  694.5 10.6 %gather_fusion = bf16[8,3,128,512]{3,2,1,0:T(8,128)(2,1)} fusion(bf16[64,3,128,512]{3,2,1,0:T(8,128)(2,1)} %get-tuple-element.178, s32[1024]{0:T(1024)S(1)} %pad_clamp_fusion.1), kind=kCustom, calls=%fused_computation | custom fusion | bytes 6291488 | tf_op jit(solution)/shard_map/while/body/eval_jaxpr/cond/branch_1_fun/gather | solution.py:47
  705.1 5.2 fusion.5
  711.8 26.2 %conditional.2 = (f32[96,128,128]{2,1,0:T(8,128)}) conditional(s32[]{:T(128)} %convert_element_type.20, f32[96,128,128]{2,1,0:T(8,128)} %get-tuple-element.313, (pred[8]{0:T(512)(128)(4,1)S(1)}, s32[]{:T(128)}, s32[96]{0:T(128)S(1)}, bf16[64,3,128,512]{3,2,1,0:T(8,128)(2,1)}, s32[64,3]{1,0:T(8,128)S(1)}, /*index=5*/s32[96]{0:T(128)S(1)}, ...), branch_computations={%region_2.0_spmd, %region_3.3_spmd} | conditional | flops 412223712 | bytes 26748024 | solution.py:66
  712.5 2.5 gather_fusion.3
  715.5 6.7 fusion
  722.2 10.6 %gather_fusion = bf16[8,3,128,512]{3,2,1,0:T(8,128)(2,1)} fusion(bf16[64,3,128,512]{3,2,1,0:T(8,128)(2,1)} %get-tuple-element.178, s32[1024]{0:T(1024)S(1)} %pad_clamp_fusion.1), kind=kCustom, calls=%fused_computation | custom fusion | bytes 6291488 | tf_op jit(solution)/shard_map/while/body/eval_jaxpr/cond/branch_1_fun/gather | solution.py:47
  732.8 5.2 fusion.5
  738.0 0.8 fusion.15
  739.4 26.3 %conditional.2 = (f32[96,128,128]{2,1,0:T(8,128)}) conditional(s32[]{:T(128)} %convert_element_type.20, f32[96,128,128]{2,1,0:T(8,128)} %get-tuple-element.313, (pred[8]{0:T(512)(128)(4,1)S(1)}, s32[]{:T(128)}, s32[96]{0:T(128)S(1)}, bf16[64,3,128,512]{3,2,1,0:T(8,128)(2,1)}, s32[64,3]{1,0:T(8,128)S(1)}, /*index=5*/s32[96]{0:T(128)S(1)}, ...), branch_computations={%region_2.0_spmd, %region_3.3_spmd} | conditional | flops 412223712 | bytes 26748024 | solution.py:66
  740.1 2.5 gather_fusion.3
  743.1 6.7 fusion
  749.9 10.6 %gather_fusion = bf16[8,3,128,512]{3,2,1,0:T(8,128)(2,1)} fusion(bf16[64,3,128,512]{3,2,1,0:T(8,128)(2,1)} %get-tuple-element.178, s32[1024]{0:T(1024)S(1)} %pad_clamp_fusion.1), kind=kCustom, calls=%fused_computation | custom fusion | bytes 6291488 | tf_op jit(solution)/shard_map/while/body/eval_jaxpr/cond/branch_1_fun/gather | solution.py:47
  760.5 5.2 fusion.5
  765.7 0.8 fusion.15
  767.1 26.2 %conditional.2 = (f32[96,128,128]{2,1,0:T(8,128)}) conditional(s32[]{:T(128)} %convert_element_type.20, f32[96,128,128]{2,1,0:T(8,128)} %get-tuple-element.313, (pred[8]{0:T(512)(128)(4,1)S(1)}, s32[]{:T(128)}, s32[96]{0:T(128)S(1)}, bf16[64,3,128,512]{3,2,1,0:T(8,128)(2,1)}, s32[64,3]{1,0:T(8,128)S(1)}, /*index=5*/s32[96]{0:T(128)S(1)}, ...), branch_computations={%region_2.0_spmd, %region_3.3_spmd} | conditional | flops 412223712 | bytes 26748024 | solution.py:66
  767.8 2.5 gather_fusion.3
  770.8 6.7 fusion
  777.5 10.6 %gather_fusion = bf16[8,3,128,512]{3,2,1,0:T(8,128)(2,1)} fusion(bf16[64,3,128,512]{3,2,1,0:T(8,128)(2,1)} %get-tuple-element.178, s32[1024]{0:T(1024)S(1)} %pad_clamp_fusion.1), kind=kCustom, calls=%fused_computation | custom fusion | bytes 6291488 | tf_op jit(solution)/shard_map/while/body/eval_jaxpr/cond/branch_1_fun/gather | solution.py:47
  788.1 5.2 fusion.5
  793.3 0.8 fusion.15
  794.8 0.8 fusion.15
  796.2 0.8 fusion.15
  797.7 0.8 fusion.15
  799.2 0.8 fusion.15
  800.6 0.8 fusion.15
  803.4 216.8 %reduce-scatter.2.cloned.1.call-done = f32[24,128,128]{2,1,0:T(8,128)} async-done(((f32[96,128,128]{2,1,0:T(8,128)}), f32[24,128,128]{2,1,0:T(8,128)}) %reduce-scatter.2.cloned.1.call-update) | async-done | bytes 1572880 | tf_op jit(solution)/shard_map/reduce_scatter | solution.py:69
  1020.2 3.1 divide_select_fusion
  (67 shorter events, 9.6 us)
Async XLA Ops:
  6.5 795.7 %copy-start = (f32[8192]{0:T(1024)S(1)}, f32[8192]{0:T(1024)}, u32[]{:S(2)}) copy-start(f32[8192]{0:T(1024)} %param.20) | copy-start | bytes 98308
  16.0 16.2 %copy-start.6 = (s32[64,3]{0,1:T(4,128)S(1)}, s32[64,3]{0,1:T(4,128)}, u32[]{:S(2)}) copy-start(s32[64,3]{0,1:T(4,128)} %param.14) | copy-start | bytes 2308
  16.0 607.8 %all-to-all-start = ((bf16[64,1,3,128,512]{4,3,2,1,0:T(8,128)(2,1)}), bf16[64,1,3,128,512]{4,3,2,1,0:T(8,128)(2,1)}, u32[]{:S(2)}, u32[]{:S(2)}) async-start(bf16[64,1,3,128,512]{4,3,2,1,0:T(8,128)(2,1)} %stack.2), calls=%async_computation | async-start | bytes 50331648 | tf_op jit(solution)/shard_map/all_to_all | solution.py:28
  31.5 988.7 %reduce-scatter.2.cloned.1.call-start = ((), (), s32[]{:S(2)}) async-start(), calls=%async_computation.2 | async-start | bytes 7864320 | tf_op jit(solution)/shard_map/reduce_scatter | solution.py:69
  623.8 3.5 copy-start.1
  623.8 3.5 copy-start.2
  623.8 3.5 copy-start.4
  623.8 3.5 copy-start.5
  802.1 0.8 copy-start.3
Sparse Core Ops, SparseCore 0:
  802.2 217.9 reduce-scatter.1
